TPU v7x, 512 devices: a whole 4x4x16 slice. The times are simulated.
512 devices in a mesh: ctx: 16 (over z_lo, core), head: 8 (over x, z_hi), dp: 4 (over y).
Axes of the slice: x: 4, y: 4, z: 16 (z_hi: 2, z_lo: 8; z = z_hi * 8 + z_lo), core: 2. Of those that a mesh axis runs over, the one named last changes fastest.
Arguments:
- queries: bfloat16 [8192, 4096], P(('dp', 'ctx'), 'head'), parts along dimension 0, may hold values from -6 to 6
- key_rows: bfloat16 [8192, 4096], P(('dp', 'ctx'), 'head'), parts along dimension 0, may hold values from -6 to 6
- value_rows: bfloat16 [8192, 4096], P(('dp', 'ctx'), 'head'), parts along dimension 0, may hold values from -6 to 6
- gate_values: bfloat16 [8192, 4096], P(('dp', 'ctx'), 'head'), parts along dimension 0, may hold values from -6 to 6
- cotangent: bfloat16 [8192, 4096], P(('dp', 'ctx'), 'head'), parts along dimension 0, may hold values from -6 to 6
- decay_rates: float32 [16, 4096], P(None, 'head'), may hold values from 0 to 1, as said below
- residues: float32 [16, 4096], P(None, 'head'), may hold values from -4 to 4
- skip_gain: float32 [4096], P('head'), may hold values from -6 to 6
Outputs:
- queries_adjoint: bfloat16 [8192, 4096], P(('dp', 'ctx'), 'head'), parts along dimension 0
- keys_adjoint: bfloat16 [8192, 4096], P(('dp', 'ctx'), 'head'), parts along dimension 0
- values_adjoint: bfloat16 [8192, 4096], P(('dp', 'ctx'), 'head'), parts along dimension 0
- gate_adjoint: bfloat16 [8192, 4096], P(('dp', 'ctx'), 'head'), parts along dimension 0
- residues_adjoint: float32 [64, 4096], P('dp', 'head'), parts along dimension 0
There are 4 independent parts, one for each index of `dp`. A program takes and returns all parts, laid end to end along the dimension named above; an argument that names none is the same for every part. Nothing has to cross between parts.
Inputs may be any that keep to these rules, and one draw needn't show every extreme that they name: `decay_rates`: every rate lies between 0.6 / 2048 and 1/16 per position.
All inputs are finite; a program needn't handle non-finite values.
Results may differ from a plain program's by a relative error of at most 0.0094.
Values may be sent and summed in bfloat16 or wider, within the bound.
No kernel may reach another device: no remote copies, remote signals or barrier semaphores. Data moves between devices by JAX's collectives and lax.ppermute only.
A program may use at most 64 MiB of HBM per device.

v0:
```python
import math
import jax
import jax.numpy as jnp
from jax import lax
from jax.sharding import PartitionSpec as P

HEAD = 128
WIN = 4


def passed_along(array, axis, by):
    length = lax.axis_size(axis)
    return lax.ppermute(array, axis, [(i, (i + by) % length) for i in range(length)])


def window_mask(row_count):
    row_ids = jnp.arange(row_count)[:, None, None]
    lag_ids = jnp.arange(WIN + 1)[None, :, None]
    column_ids = jnp.arange(row_count)[None, None, :]
    return ((lag_ids > 0) | (column_ids <= row_ids)) & ((lag_ids < WIN) | (column_ids > row_ids))


def local(queries, key_rows, value_rows, gate_values, cotangent, decay_rates, residues, skip_gain):
    members = lax.axis_size("ctx")
    tok_rows, channels = queries.shape
    local_heads = channels // HEAD
    scale_factor = 1.0 / math.sqrt(HEAD)
    weights = jnp.sqrt(-jnp.expm1(-2.0 * decay_rates))
    mixing = residues * weights
    loop_gap = -jnp.expm1(-decay_rates * (tok_rows * members))
    device_decay = jnp.exp(-decay_rates * tok_rows)
    piece_rows = min(128, tok_rows)
    pieces = tok_rows // piece_rows
    offsets = jnp.arange(piece_rows, dtype=jnp.float32)[:, None, None]
    piece_index = jnp.arange(pieces, dtype=jnp.float32)[:, None, None]
    start_weights = jnp.exp(-decay_rates[None] * offsets)
    growth = jnp.exp(decay_rates[None] * offsets)
    delta_rows = cotangent.astype(jnp.float32) * gate_values.astype(jnp.float32)
    blocks_delta = delta_rows.reshape(pieces, piece_rows, channels)
    piece_starts = jnp.einsum(
        "qpc,mqc->mpc", start_weights, blocks_delta, precision=lax.Precision.HIGHEST
    )
    head_state = jnp.sum(
        jnp.exp(-decay_rates[None] * (piece_index * piece_rows)) * piece_starts, axis=0
    )

    def backward_turn(turn_index, moving):
        return passed_along(device_decay * moving + head_state, "ctx", -1)

    incoming = lax.fori_loop(0, members, backward_turn, jnp.zeros_like(head_state)) / loop_gap

    def backward_step(carried, segment):
        local_part = growth * lax.cumsum(start_weights * segment[:, None, :], axis=0, reverse=True)
        states = local_part + jnp.exp(-decay_rates[None] * (piece_rows - offsets)) * carried[None]
        mixture = jnp.sum(mixing[None] * states, axis=1) + skip_gain[None] * segment
        return (states[0], mixture)

    unused_state, adjoint_rows = lax.scan(backward_step, incoming, blocks_delta, reverse=True)
    attended_adjoint = adjoint_rows.reshape(tok_rows, channels).astype(jnp.bfloat16)
    key_value = jnp.stack([key_rows, value_rows])
    window = [key_value]
    moving = key_value
    for lag_index in range(WIN):
        moving = passed_along(moving, "ctx", 1)
        window.append(moving)
    stacked = jnp.stack(window)
    key_window = stacked[:, 0]
    value_window = stacked[:, 1]
    allowed = window_mask(tok_rows)
    attended_parts = []
    query_adjoints = []
    key_partials = []
    value_partials = []
    for head_index in range(local_heads):
        first = head_index * HEAD
        query_head = queries[:, first : first + HEAD]
        key_head = key_window[:, :, first : first + HEAD]
        value_head = value_window[:, :, first : first + HEAD]
        adjoint_head = attended_adjoint[:, first : first + HEAD]
        scores = (
            jnp.einsum("re,kse->rks", query_head, key_head, preferred_element_type=jnp.float32)
            * scale_factor
        )
        masked = jnp.where(allowed, scores, -jnp.inf)
        row_top = jnp.max(masked, axis=(1, 2), keepdims=True)
        raised = jnp.exp(masked - row_top)
        probability = raised / jnp.sum(raised, axis=(1, 2), keepdims=True)
        rounded_prob = probability.astype(jnp.bfloat16)
        attended_parts.append(
            jnp.einsum(
                "rks,kse->re", rounded_prob, value_head, preferred_element_type=jnp.float32
            ).astype(jnp.bfloat16)
        )
        weight_adjoint = jnp.einsum(
            "re,kse->rks", adjoint_head, value_head, preferred_element_type=jnp.float32
        )
        inner_sum = jnp.sum(probability * weight_adjoint, axis=(1, 2), keepdims=True)
        score_adjoint = (probability * (weight_adjoint - inner_sum) * scale_factor).astype(
            jnp.bfloat16
        )
        query_adjoints.append(
            jnp.einsum(
                "rks,kse->re", score_adjoint, key_head, preferred_element_type=jnp.float32
            ).astype(jnp.bfloat16)
        )
        key_partials.append(
            jnp.einsum(
                "rks,re->kse", score_adjoint, query_head, preferred_element_type=jnp.float32
            ).astype(jnp.bfloat16)
        )
        value_partials.append(
            jnp.einsum(
                "rks,re->kse", rounded_prob, adjoint_head, preferred_element_type=jnp.float32
            ).astype(jnp.bfloat16)
        )
    attended = jnp.concatenate(attended_parts, axis=1)
    queries_adjoint = jnp.concatenate(query_adjoints, axis=1)
    partials = jnp.stack(
        [jnp.concatenate(key_partials, axis=2), jnp.concatenate(value_partials, axis=2)], axis=1
    )
    collected = partials[0].astype(jnp.float32)
    for lag_index in range(1, WIN + 1):
        collected = collected + passed_along(partials[lag_index], "ctx", -lag_index).astype(
            jnp.float32
        )
    keys_adjoint = collected[0].astype(jnp.bfloat16)
    values_adjoint = collected[1].astype(jnp.bfloat16)
    signal = attended.astype(jnp.float32)
    blocks_signal = signal.reshape(pieces, piece_rows, channels)
    end_weights = jnp.exp(-decay_rates[None] * (piece_rows - 1.0 - offsets))
    piece_ends = jnp.einsum(
        "qpc,mqc->mpc", end_weights, blocks_signal, precision=lax.Precision.HIGHEST
    )
    tail_state = jnp.sum(
        jnp.exp(-decay_rates[None] * ((pieces - 1.0 - piece_index) * piece_rows)) * piece_ends,
        axis=0,
    )

    def forward_turn(turn_index, moving):
        return passed_along(device_decay * moving + tail_state, "ctx", 1)

    arriving = lax.fori_loop(0, members, forward_turn, jnp.zeros_like(tail_state)) / loop_gap
    entering = jnp.exp(-decay_rates[None] * (offsets + 1.0))

    def forward_step(carried, step_item):
        segment, matched = step_item
        local_part = start_weights * jnp.cumsum(growth * segment[:, None, :], axis=0)
        states = local_part + entering * carried[None]
        mixture = jnp.sum(mixing[None] * states, axis=1) + skip_gain[None] * segment
        product = jnp.sum(weights[None] * matched[:, None, :] * states, axis=0)
        return (states[-1], (mixture, product))

    closing, (mixed_rows, products) = lax.scan(
        forward_step, arriving, (blocks_signal, blocks_delta)
    )
    gate_adjoint = (cotangent.astype(jnp.float32) * mixed_rows.reshape(tok_rows, channels)).astype(
        jnp.bfloat16
    )
    residues_adjoint = lax.psum(jnp.sum(products, axis=0), "ctx")
    return (queries_adjoint, keys_adjoint, values_adjoint, gate_adjoint, residues_adjoint)


def solution(mesh):
    in_specs = (
        P(("dp", "ctx"), "head"),
        P(("dp", "ctx"), "head"),
        P(("dp", "ctx"), "head"),
        P(("dp", "ctx"), "head"),
        P(("dp", "ctx"), "head"),
        P(None, "head"),
        P(None, "head"),
        P("head"),
    )
    out_specs = (
        P(("dp", "ctx"), "head"),
        P(("dp", "ctx"), "head"),
        P(("dp", "ctx"), "head"),
        P(("dp", "ctx"), "head"),
        P("dp", "head"),
    )
    return jax.shard_map(local, mesh=mesh, in_specs=in_specs, out_specs=out_specs, check_vma=False)
```

profile of v0, /device:TPU:30, one launch (start us, length us, event | category | flops | bytes accessed | tf_op | source)
XLA Modules:
  0.0 588.1 jit_solution(3463437683806566200)
XLA Ops:
  5.4 11.1 %fusion.2 = f32[128,16,512]{2,1,0:T(8,128)} fusion(f32[128,512]{1,0:T(8,128)S(1)} %get-tuple-element.151, f32[16,512]{1,0:T(8,128)S(1)} %get-tuple-element.163), kind=kOutput, calls=%fused_computation.10 | output fusion | flops 135266304 | bytes 4489216 | tf_op jit(solution)/shard_map/while/body/eval_jaxpr/reduce_window_sum | solution.py:53
  21.2 12.1 %collective-permute-done.3 = bf16[2,128,512]{2,1,0:T(8,128)(2,1)S(1)} collective-permute-done((bf16[2,128,512]{2,1,0:T(8,128)(2,1)S(1)}, bf16[2,128,512]{2,1,0:T(8,128)(2,1)S(1)}, u32[]{:S(2)}, u32[]{:S(2)}) %collective-permute-start.3) | collective-permute-done | bytes 262176 | tf_op jit(solution)/shard_map/ppermute | solution.py:13
  35.7 11.8 %collective-permute-done.4 = bf16[2,128,512]{2,1,0:T(8,128)(2,1)S(1)} collective-permute-done((bf16[2,128,512]{2,1,0:T(8,128)(2,1)S(1)}, bf16[2,128,512]{2,1,0:T(8,128)(2,1)S(1)}, u32[]{:S(2)}, u32[]{:S(2)}) %collective-permute-start.4) | collective-permute-done | bytes 262176 | tf_op jit(solution)/shard_map/ppermute | solution.py:13
  49.7 12.6 %collective-permute-done.5 = bf16[2,128,512]{2,1,0:T(8,128)(2,1)S(1)} collective-permute-done((bf16[2,128,512]{2,1,0:T(8,128)(2,1)S(1)}, bf16[2,128,512]{2,1,0:T(8,128)(2,1)S(1)}, u32[]{:S(2)}, u32[]{:S(2)}) %collective-permute-start.5) | collective-permute-done | bytes 262176 | tf_op jit(solution)/shard_map/ppermute | solution.py:13
  68.1 181.3 %while.4 = (s32[]{:T(128)}, f32[16,512]{1,0:T(8,128)S(1)}, f32[16,512]{1,0:T(8,128)S(1)}, f32[16,512]{1,0:T(8,128)S(1)}, s32[]{:T(128)}) while((s32[]{:T(128)}, f32[16,512]{1,0:T(8,128)S(1)}, f32[16,512]{1,0:T(8,128)S(1)}, f32[16,512]{1,0:T(8,128)S(1)}, s32[]{:T(128)}) %tuple.67), condition=%wide.region_4.0_spmd, body=%wide.region_3.4_spmd.sunk | while | flops 16386 | bytes 262245 | solution.py:50
  71.6 10.3 %collective-permute-start = (f32[16,512]{1,0:T(8,128)S(1)}, f32[16,512]{1,0:T(8,128)S(1)}, u32[]{:S(2)}, u32[]{:S(2)}) collective-permute-start(f32[16,512]{1,0:T(8,128)S(1)} %multiply_add_fusion.5), channel_id=1, source_target_pairs={{0,480},{32,0},{64,32},{96,64},{128,96},{160,128},{192,160},{224,1... | collective-permute-start | bytes 98312 | tf_op jit(solution)/shard_map/while/body/eval_jaxpr/ppermute | solution.py:13
  83.5 10.3 %collective-permute-start = (f32[16,512]{1,0:T(8,128)S(1)}, f32[16,512]{1,0:T(8,128)S(1)}, u32[]{:S(2)}, u32[]{:S(2)}) collective-permute-start(f32[16,512]{1,0:T(8,128)S(1)} %multiply_add_fusion.5), channel_id=1, source_target_pairs={{0,480},{32,0},{64,32},{96,64},{128,96},{160,128},{192,160},{224,1... | collective-permute-start | bytes 98312 | tf_op jit(solution)/shard_map/while/body/eval_jaxpr/ppermute | solution.py:13
  95.3 10.3 %collective-permute-start = (f32[16,512]{1,0:T(8,128)S(1)}, f32[16,512]{1,0:T(8,128)S(1)}, u32[]{:S(2)}, u32[]{:S(2)}) collective-permute-start(f32[16,512]{1,0:T(8,128)S(1)} %multiply_add_fusion.5), channel_id=1, source_target_pairs={{0,480},{32,0},{64,32},{96,64},{128,96},{160,128},{192,160},{224,1... | collective-permute-start | bytes 98312 | tf_op jit(solution)/shard_map/while/body/eval_jaxpr/ppermute | solution.py:13
  107.2 10.3 %collective-permute-start = (f32[16,512]{1,0:T(8,128)S(1)}, f32[16,512]{1,0:T(8,128)S(1)}, u32[]{:S(2)}, u32[]{:S(2)}) collective-permute-start(f32[16,512]{1,0:T(8,128)S(1)} %multiply_add_fusion.5), channel_id=1, source_target_pairs={{0,480},{32,0},{64,32},{96,64},{128,96},{160,128},{192,160},{224,1... | collective-permute-start | bytes 98312 | tf_op jit(solution)/shard_map/while/body/eval_jaxpr/ppermute | solution.py:13
  119.0 10.3 %collective-permute-start = (f32[16,512]{1,0:T(8,128)S(1)}, f32[16,512]{1,0:T(8,128)S(1)}, u32[]{:S(2)}, u32[]{:S(2)}) collective-permute-start(f32[16,512]{1,0:T(8,128)S(1)} %multiply_add_fusion.5), channel_id=1, source_target_pairs={{0,480},{32,0},{64,32},{96,64},{128,96},{160,128},{192,160},{224,1... | collective-permute-start | bytes 98312 | tf_op jit(solution)/shard_map/while/body/eval_jaxpr/ppermute | solution.py:13
  130.9 10.3 %collective-permute-start = (f32[16,512]{1,0:T(8,128)S(1)}, f32[16,512]{1,0:T(8,128)S(1)}, u32[]{:S(2)}, u32[]{:S(2)}) collective-permute-start(f32[16,512]{1,0:T(8,128)S(1)} %multiply_add_fusion.5), channel_id=1, source_target_pairs={{0,480},{32,0},{64,32},{96,64},{128,96},{160,128},{192,160},{224,1... | collective-permute-start | bytes 98312 | tf_op jit(solution)/shard_map/while/body/eval_jaxpr/ppermute | solution.py:13
  142.7 10.3 %collective-permute-start = (f32[16,512]{1,0:T(8,128)S(1)}, f32[16,512]{1,0:T(8,128)S(1)}, u32[]{:S(2)}, u32[]{:S(2)}) collective-permute-start(f32[16,512]{1,0:T(8,128)S(1)} %multiply_add_fusion.5), channel_id=1, source_target_pairs={{0,480},{32,0},{64,32},{96,64},{128,96},{160,128},{192,160},{224,1... | collective-permute-start | bytes 98312 | tf_op jit(solution)/shard_map/while/body/eval_jaxpr/ppermute | solution.py:13
  154.6 10.3 %collective-permute-start = (f32[16,512]{1,0:T(8,128)S(1)}, f32[16,512]{1,0:T(8,128)S(1)}, u32[]{:S(2)}, u32[]{:S(2)}) collective-permute-start(f32[16,512]{1,0:T(8,128)S(1)} %multiply_add_fusion.5), channel_id=1, source_target_pairs={{0,480},{32,0},{64,32},{96,64},{128,96},{160,128},{192,160},{224,1... | collective-permute-start | bytes 98312 | tf_op jit(solution)/shard_map/while/body/eval_jaxpr/ppermute | solution.py:13
  166.4 10.3 %collective-permute-start = (f32[16,512]{1,0:T(8,128)S(1)}, f32[16,512]{1,0:T(8,128)S(1)}, u32[]{:S(2)}, u32[]{:S(2)}) collective-permute-start(f32[16,512]{1,0:T(8,128)S(1)} %multiply_add_fusion.5), channel_id=1, source_target_pairs={{0,480},{32,0},{64,32},{96,64},{128,96},{160,128},{192,160},{224,1... | collective-permute-start | bytes 98312 | tf_op jit(solution)/shard_map/while/body/eval_jaxpr/ppermute | solution.py:13
  178.3 10.3 %collective-permute-start = (f32[16,512]{1,0:T(8,128)S(1)}, f32[16,512]{1,0:T(8,128)S(1)}, u32[]{:S(2)}, u32[]{:S(2)}) collective-permute-start(f32[16,512]{1,0:T(8,128)S(1)} %multiply_add_fusion.5), channel_id=1, source_target_pairs={{0,480},{32,0},{64,32},{96,64},{128,96},{160,128},{192,160},{224,1... | collective-permute-start | bytes 98312 | tf_op jit(solution)/shard_map/while/body/eval_jaxpr/ppermute | solution.py:13
  190.1 10.3 %collective-permute-start = (f32[16,512]{1,0:T(8,128)S(1)}, f32[16,512]{1,0:T(8,128)S(1)}, u32[]{:S(2)}, u32[]{:S(2)}) collective-permute-start(f32[16,512]{1,0:T(8,128)S(1)} %multiply_add_fusion.5), channel_id=1, source_target_pairs={{0,480},{32,0},{64,32},{96,64},{128,96},{160,128},{192,160},{224,1... | collective-permute-start | bytes 98312 | tf_op jit(solution)/shard_map/while/body/eval_jaxpr/ppermute | solution.py:13
  202.0 10.3 %collective-permute-start = (f32[16,512]{1,0:T(8,128)S(1)}, f32[16,512]{1,0:T(8,128)S(1)}, u32[]{:S(2)}, u32[]{:S(2)}) collective-permute-start(f32[16,512]{1,0:T(8,128)S(1)} %multiply_add_fusion.5), channel_id=1, source_target_pairs={{0,480},{32,0},{64,32},{96,64},{128,96},{160,128},{192,160},{224,1... | collective-permute-start | bytes 98312 | tf_op jit(solution)/shard_map/while/body/eval_jaxpr/ppermute | solution.py:13
  213.9 10.3 %collective-permute-start = (f32[16,512]{1,0:T(8,128)S(1)}, f32[16,512]{1,0:T(8,128)S(1)}, u32[]{:S(2)}, u32[]{:S(2)}) collective-permute-start(f32[16,512]{1,0:T(8,128)S(1)} %multiply_add_fusion.5), channel_id=1, source_target_pairs={{0,480},{32,0},{64,32},{96,64},{128,96},{160,128},{192,160},{224,1... | collective-permute-start | bytes 98312 | tf_op jit(solution)/shard_map/while/body/eval_jaxpr/ppermute | solution.py:13
  225.7 10.3 %collective-permute-start = (f32[16,512]{1,0:T(8,128)S(1)}, f32[16,512]{1,0:T(8,128)S(1)}, u32[]{:S(2)}, u32[]{:S(2)}) collective-permute-start(f32[16,512]{1,0:T(8,128)S(1)} %multiply_add_fusion.5), channel_id=1, source_target_pairs={{0,480},{32,0},{64,32},{96,64},{128,96},{160,128},{192,160},{224,1... | collective-permute-start | bytes 98312 | tf_op jit(solution)/shard_map/while/body/eval_jaxpr/ppermute | solution.py:13
  237.6 10.3 %collective-permute-start = (f32[16,512]{1,0:T(8,128)S(1)}, f32[16,512]{1,0:T(8,128)S(1)}, u32[]{:S(2)}, u32[]{:S(2)}) collective-permute-start(f32[16,512]{1,0:T(8,128)S(1)} %multiply_add_fusion.5), channel_id=1, source_target_pairs={{0,480},{32,0},{64,32},{96,64},{128,96},{160,128},{192,160},{224,1... | collective-permute-start | bytes 98312 | tf_op jit(solution)/shard_map/while/body/eval_jaxpr/ppermute | solution.py:13
  249.4 189.8 %while.5 = (s32[]{:T(128)}, f32[16,512]{1,0:T(8,128)S(1)}, f32[16,512]{1,0:T(8,128)S(1)}, f32[16,512]{1,0:T(8,128)S(1)}, s32[]{:T(128)}) while((s32[]{:T(128)}, f32[16,512]{1,0:T(8,128)S(1)}, f32[16,512]{1,0:T(8,128)S(1)}, f32[16,512]{1,0:T(8,128)S(1)}, s32[]{:T(128)}) %tuple.73), condition=%wide.region_18.19_spmd, body=%wide.region_17.18_spmd.sunk | while | flops 16386 | bytes 262245 | solution.py:142
  429.2 10.0 %collective-permute-done.1 = f32[16,512]{1,0:T(8,128)S(1)} collective-permute-done((f32[16,512]{1,0:T(8,128)S(1)}, f32[16,512]{1,0:T(8,128)S(1)}, u32[]{:S(2)}, u32[]{:S(2)}) %collective-permute-start.1) | collective-permute-done | bytes 32800 | tf_op jit(solution)/shard_map/while/body/eval_jaxpr/ppermute | solution.py:13
  439.4 29.8 %multiply_reduce_fusion.2 = (f32[16,512]{1,0:T(8,128)S(1)}, f32[128,512]{1,0:T(8,128)S(1)}, f32[128,512]{1,0:T(8,128)S(1)}) fusion(f32[16,512]{1,0:T(8,128)S(1)} %get-tuple-element.160, f32[128,512]{1,0:T(8,128)S(1)} %get-tuple-element.151, f32[16,512]{1,0:T(8,128)S(1)} %get-tuple-element.159, f32[16,512]{1,0:T(8,128)S(1)} %get-tuple-element.157, ...), kind=kOutput, calls=%fused_computation.4 | output fusion | flops 152952832 | bytes 5473280 | tf_op jit(solution)/shard_map/while/body/eval_jaxpr/jit(cumsum)/reduce_window_sum | solution.py:147
  484.0 101.4 %psum.7 = f32[16,512]{1,0:T(8,128)} all-reduce(f32[16,512]{1,0:T(8,128)S(1)} %get-tuple-element.122), channel_id=1, replica_groups=mesh['ctx'=16,'head'=8,'dp'=4] {'ctx'}, use_global_device_ids=true, to_apply=%region_21.22 | all-reduce | flops 8192 | bytes 65536 | tf_op jit(solution)/shard_map/psum | solution.py:159
  (190 shorter events, 243.8 us)
Async XLA Ops:
  1.7 16.6 %collective-permute-start.2 = (bf16[2,128,512]{2,1,0:T(8,128)(2,1)S(1)}, bf16[2,128,512]{2,1,0:T(8,128)(2,1)S(1)}, u32[]{:S(2)}, u32[]{:S(2)}) collective-permute-start(bf16[2,128,512]{2,1,0:T(8,128)(2,1)S(1)} %pad_maximum_fusion.1), channel_id=1, source_target_pairs={{0,32},{32,64},{64,96},{96,128},{128,160},{160,192},{192,224},{224... | collective-permute-start | bytes 786440 | tf_op jit(solution)/shard_map/ppermute | solution.py:13
  18.3 14.9 %collective-permute-start.3 = (bf16[2,128,512]{2,1,0:T(8,128)(2,1)S(1)}, bf16[2,128,512]{2,1,0:T(8,128)(2,1)S(1)}, u32[]{:S(2)}, u32[]{:S(2)}) collective-permute-start(bf16[2,128,512]{2,1,0:T(8,128)(2,1)S(1)} %collective-permute-done.2), channel_id=1, source_target_pairs={{0,32},{32,64},{64,96},{96,128},{128,160},{160,192},{192,224},{224... | collective-permute-start | bytes 786440 | tf_op jit(solution)/shard_map/ppermute | solution.py:13
  33.2 14.3 %collective-permute-start.4 = (bf16[2,128,512]{2,1,0:T(8,128)(2,1)S(1)}, bf16[2,128,512]{2,1,0:T(8,128)(2,1)S(1)}, u32[]{:S(2)}, u32[]{:S(2)}) collective-permute-start(bf16[2,128,512]{2,1,0:T(8,128)(2,1)S(1)} %collective-permute-done.3), channel_id=1, source_target_pairs={{0,32},{32,64},{64,96},{96,128},{128,160},{160,192},{192,224},{224... | collective-permute-start | bytes 786440 | tf_op jit(solution)/shard_map/ppermute | solution.py:13
  47.5 14.8 %collective-permute-start.5 = (bf16[2,128,512]{2,1,0:T(8,128)(2,1)S(1)}, bf16[2,128,512]{2,1,0:T(8,128)(2,1)S(1)}, u32[]{:S(2)}, u32[]{:S(2)}) collective-permute-start(bf16[2,128,512]{2,1,0:T(8,128)(2,1)S(1)} %collective-permute-done.4), channel_id=1, source_target_pairs={{0,32},{32,64},{64,96},{96,128},{128,160},{160,192},{192,224},{224... | collective-permute-start | bytes 786440 | tf_op jit(solution)/shard_map/ppermute | solution.py:13
  71.6 11.8 %collective-permute-start = (f32[16,512]{1,0:T(8,128)S(1)}, f32[16,512]{1,0:T(8,128)S(1)}, u32[]{:S(2)}, u32[]{:S(2)}) collective-permute-start(f32[16,512]{1,0:T(8,128)S(1)} %multiply_add_fusion.5), channel_id=1, source_target_pairs={{0,480},{32,0},{64,32},{96,64},{128,96},{160,128},{192,160},{224,1... | collective-permute-start | bytes 98312 | tf_op jit(solution)/shard_map/while/body/eval_jaxpr/ppermute | solution.py:13
  83.5 11.8 %collective-permute-start = (f32[16,512]{1,0:T(8,128)S(1)}, f32[16,512]{1,0:T(8,128)S(1)}, u32[]{:S(2)}, u32[]{:S(2)}) collective-permute-start(f32[16,512]{1,0:T(8,128)S(1)} %multiply_add_fusion.5), channel_id=1, source_target_pairs={{0,480},{32,0},{64,32},{96,64},{128,96},{160,128},{192,160},{224,1... | collective-permute-start | bytes 98312 | tf_op jit(solution)/shard_map/while/body/eval_jaxpr/ppermute | solution.py:13
  95.3 11.8 %collective-permute-start = (f32[16,512]{1,0:T(8,128)S(1)}, f32[16,512]{1,0:T(8,128)S(1)}, u32[]{:S(2)}, u32[]{:S(2)}) collective-permute-start(f32[16,512]{1,0:T(8,128)S(1)} %multiply_add_fusion.5), channel_id=1, source_target_pairs={{0,480},{32,0},{64,32},{96,64},{128,96},{160,128},{192,160},{224,1... | collective-permute-start | bytes 98312 | tf_op jit(solution)/shard_map/while/body/eval_jaxpr/ppermute | solution.py:13
  107.2 11.8 %collective-permute-start = (f32[16,512]{1,0:T(8,128)S(1)}, f32[16,512]{1,0:T(8,128)S(1)}, u32[]{:S(2)}, u32[]{:S(2)}) collective-permute-start(f32[16,512]{1,0:T(8,128)S(1)} %multiply_add_fusion.5), channel_id=1, source_target_pairs={{0,480},{32,0},{64,32},{96,64},{128,96},{160,128},{192,160},{224,1... | collective-permute-start | bytes 98312 | tf_op jit(solution)/shard_map/while/body/eval_jaxpr/ppermute | solution.py:13
  119.0 11.8 %collective-permute-start = (f32[16,512]{1,0:T(8,128)S(1)}, f32[16,512]{1,0:T(8,128)S(1)}, u32[]{:S(2)}, u32[]{:S(2)}) collective-permute-start(f32[16,512]{1,0:T(8,128)S(1)} %multiply_add_fusion.5), channel_id=1, source_target_pairs={{0,480},{32,0},{64,32},{96,64},{128,96},{160,128},{192,160},{224,1... | collective-permute-start | bytes 98312 | tf_op jit(solution)/shard_map/while/body/eval_jaxpr/ppermute | solution.py:13
  130.9 11.8 %collective-permute-start = (f32[16,512]{1,0:T(8,128)S(1)}, f32[16,512]{1,0:T(8,128)S(1)}, u32[]{:S(2)}, u32[]{:S(2)}) collective-permute-start(f32[16,512]{1,0:T(8,128)S(1)} %multiply_add_fusion.5), channel_id=1, source_target_pairs={{0,480},{32,0},{64,32},{96,64},{128,96},{160,128},{192,160},{224,1... | collective-permute-start | bytes 98312 | tf_op jit(solution)/shard_map/while/body/eval_jaxpr/ppermute | solution.py:13
  142.7 11.8 %collective-permute-start = (f32[16,512]{1,0:T(8,128)S(1)}, f32[16,512]{1,0:T(8,128)S(1)}, u32[]{:S(2)}, u32[]{:S(2)}) collective-permute-start(f32[16,512]{1,0:T(8,128)S(1)} %multiply_add_fusion.5), channel_id=1, source_target_pairs={{0,480},{32,0},{64,32},{96,64},{128,96},{160,128},{192,160},{224,1... | collective-permute-start | bytes 98312 | tf_op jit(solution)/shard_map/while/body/eval_jaxpr/ppermute | solution.py:13
  154.6 11.8 %collective-permute-start = (f32[16,512]{1,0:T(8,128)S(1)}, f32[16,512]{1,0:T(8,128)S(1)}, u32[]{:S(2)}, u32[]{:S(2)}) collective-permute-start(f32[16,512]{1,0:T(8,128)S(1)} %multiply_add_fusion.5), channel_id=1, source_target_pairs={{0,480},{32,0},{64,32},{96,64},{128,96},{160,128},{192,160},{224,1... | collective-permute-start | bytes 98312 | tf_op jit(solution)/shard_map/while/body/eval_jaxpr/ppermute | solution.py:13
  166.4 11.8 %collective-permute-start = (f32[16,512]{1,0:T(8,128)S(1)}, f32[16,512]{1,0:T(8,128)S(1)}, u32[]{:S(2)}, u32[]{:S(2)}) collective-permute-start(f32[16,512]{1,0:T(8,128)S(1)} %multiply_add_fusion.5), channel_id=1, source_target_pairs={{0,480},{32,0},{64,32},{96,64},{128,96},{160,128},{192,160},{224,1... | collective-permute-start | bytes 98312 | tf_op jit(solution)/shard_map/while/body/eval_jaxpr/ppermute | solution.py:13
  178.3 11.8 %collective-permute-start = (f32[16,512]{1,0:T(8,128)S(1)}, f32[16,512]{1,0:T(8,128)S(1)}, u32[]{:S(2)}, u32[]{:S(2)}) collective-permute-start(f32[16,512]{1,0:T(8,128)S(1)} %multiply_add_fusion.5), channel_id=1, source_target_pairs={{0,480},{32,0},{64,32},{96,64},{128,96},{160,128},{192,160},{224,1... | collective-permute-start | bytes 98312 | tf_op jit(solution)/shard_map/while/body/eval_jaxpr/ppermute | solution.py:13
  190.1 11.8 %collective-permute-start = (f32[16,512]{1,0:T(8,128)S(1)}, f32[16,512]{1,0:T(8,128)S(1)}, u32[]{:S(2)}, u32[]{:S(2)}) collective-permute-start(f32[16,512]{1,0:T(8,128)S(1)} %multiply_add_fusion.5), channel_id=1, source_target_pairs={{0,480},{32,0},{64,32},{96,64},{128,96},{160,128},{192,160},{224,1... | collective-permute-start | bytes 98312 | tf_op jit(solution)/shard_map/while/body/eval_jaxpr/ppermute | solution.py:13
  202.0 11.8 %collective-permute-start = (f32[16,512]{1,0:T(8,128)S(1)}, f32[16,512]{1,0:T(8,128)S(1)}, u32[]{:S(2)}, u32[]{:S(2)}) collective-permute-start(f32[16,512]{1,0:T(8,128)S(1)} %multiply_add_fusion.5), channel_id=1, source_target_pairs={{0,480},{32,0},{64,32},{96,64},{128,96},{160,128},{192,160},{224,1... | collective-permute-start | bytes 98312 | tf_op jit(solution)/shard_map/while/body/eval_jaxpr/ppermute | solution.py:13
  213.9 11.8 %collective-permute-start = (f32[16,512]{1,0:T(8,128)S(1)}, f32[16,512]{1,0:T(8,128)S(1)}, u32[]{:S(2)}, u32[]{:S(2)}) collective-permute-start(f32[16,512]{1,0:T(8,128)S(1)} %multiply_add_fusion.5), channel_id=1, source_target_pairs={{0,480},{32,0},{64,32},{96,64},{128,96},{160,128},{192,160},{224,1... | collective-permute-start | bytes 98312 | tf_op jit(solution)/shard_map/while/body/eval_jaxpr/ppermute | solution.py:13
  249.4 11.8 %collective-permute-start.1 = (f32[16,512]{1,0:T(8,128)S(1)}, f32[16,512]{1,0:T(8,128)S(1)}, u32[]{:S(2)}, u32[]{:S(2)}) collective-permute-start(f32[16,512]{1,0:T(8,128)S(1)} %multiply_add_fusion.6), channel_id=1, source_target_pairs={{0,32},{32,64},{64,96},{96,128},{128,160},{160,192},{192,224},{224... | collective-permute-start | bytes 98312 | tf_op jit(solution)/shard_map/while/body/eval_jaxpr/ppermute | solution.py:13
  415.3 11.9 %collective-permute-start.1 = (f32[16,512]{1,0:T(8,128)S(1)}, f32[16,512]{1,0:T(8,128)S(1)}, u32[]{:S(2)}, u32[]{:S(2)}) collective-permute-start(f32[16,512]{1,0:T(8,128)S(1)} %multiply_add_fusion.6), channel_id=1, source_target_pairs={{0,32},{32,64},{64,96},{96,128},{128,160},{160,192},{192,224},{224... | collective-permute-start | bytes 98312 | tf_op jit(solution)/shard_map/while/body/eval_jaxpr/ppermute | solution.py:13
  427.3 11.9 %collective-permute-start.1 = (f32[16,512]{1,0:T(8,128)S(1)}, f32[16,512]{1,0:T(8,128)S(1)}, u32[]{:S(2)}, u32[]{:S(2)}) collective-permute-start(f32[16,512]{1,0:T(8,128)S(1)} %multiply_add_fusion.6), channel_id=1, source_target_pairs={{0,32},{32,64},{64,96},{96,128},{128,160},{160,192},{192,224},{224... | collective-permute-start | bytes 98312 | tf_op jit(solution)/shard_map/while/body/eval_jaxpr/ppermute | solution.py:13
  475.2 110.1 %collective-permute-start.6 = (bf16[2,128,512]{1,2,0:T(8,128)(2,1)}, bf16[2,128,512]{1,2,0:T(8,128)(2,1)S(1)}, u32[]{:S(2)}, u32[]{:S(2)}) collective-permute-start(bf16[2,128,512]{1,2,0:T(8,128)(2,1)} %get-tuple-element.143), channel_id=1, source_target_pairs={{0,480},{32,0},{64,32},{96,64},{128,96},{160,128},{192,160},{224,1... | collective-permute-start | bytes 786440 | tf_op jit(solution)/shard_map/ppermute | solution.py:13
  477.2 108.2 %collective-permute-start.7 = (bf16[2,128,512]{1,2,0:T(8,128)(2,1)}, bf16[2,128,512]{1,2,0:T(8,128)(2,1)S(1)}, u32[]{:S(2)}, u32[]{:S(2)}) collective-permute-start(bf16[2,128,512]{1,2,0:T(8,128)(2,1)} %get-tuple-element.144), channel_id=1, source_target_pairs={{0,448},{32,480},{64,0},{96,32},{128,64},{160,96},{192,128},{224,1... | collective-permute-start | bytes 786440 | tf_op jit(solution)/shard_map/ppermute | solution.py:13
  479.1 106.3 %collective-permute-start.9 = (bf16[2,128,512]{1,2,0:T(8,128)(2,1)S(1)}, bf16[2,128,512]{1,2,0:T(8,128)(2,1)S(1)}, u32[]{:S(2)}, u32[]{:S(2)}) collective-permute-start(bf16[2,128,512]{1,2,0:T(8,128)(2,1)S(1)} %get-tuple-element.145), channel_id=1, source_target_pairs={{0,384},{32,416},{64,448},{96,480},{128,0},{160,32},{192,64},{224,... | collective-permute-start | bytes 786440 | tf_op jit(solution)/shard_map/ppermute | solution.py:13
  481.0 104.4 %collective-permute-start.8 = (bf16[2,128,512]{1,2,0:T(8,128)(2,1)S(1)}, bf16[2,128,512]{1,2,0:T(8,128)(2,1)}, u32[]{:S(2)}, u32[]{:S(2)}) collective-permute-start(bf16[2,128,512]{1,2,0:T(8,128)(2,1)S(1)} %get-tuple-element.146), channel_id=1, source_target_pairs={{0,416},{32,448},{64,480},{96,0},{128,32},{160,64},{192,96},{224,1... | collective-permute-start | bytes 786440 | tf_op jit(solution)/shard_map/ppermute | solution.py:13
  (34 other events, 880.8 us)
where the time goes:
time: 589 us; the launch traced here: 588 us
  waiting for transfers between devices  222 us (38%)
  starting transfers between devices  202 us (34%)
  blocking collectives  101 us (17%)
  other arithmetic  51.4 us (9%)
  matrix products  6.17 us (1%)
    ppermute x40, waiting for transfers between devices, passed_along(): lax.ppermute(array, axis, [(i, (i + by) % length) for i in range(length)])  222 us
    ppermute x40, starting transfers between devices, passed_along(): lax.ppermute(array, axis, [(i, (i + by) % length) for i in range(length)])  202 us
    psum x1, blocking collectives, local(): residues_adjoint = lax.psum(jnp.sum(products, axis=0), 'ctx')  101 us
    another operation x1, other arithmetic, forward_step(): jnp.cumsum(growth * segment[:, None, :], axis=0)  29.8 us
  transfers between devices with their start and end apart: 40, of which 36 were waited for; matrix products, arithmetic and copies ran while one was open for 3% of the time, Pallas kernels for 0%

commit v1 on v0

--- a/solution.py
+++ b/solution.py
@@ -156,7 +156,7 @@
     gate_adjoint = (cotangent.astype(jnp.float32) * mixed_rows.reshape(tok_rows, channels)).astype(
         jnp.bfloat16
     )
-    residues_adjoint = lax.psum(jnp.sum(products, axis=0), "ctx")
+    residues_adjoint = jnp.sum(lax.all_gather(jnp.sum(products, axis=0), "ctx"), axis=0)
     return (queries_adjoint, keys_adjoint, values_adjoint, gate_adjoint, residues_adjoint)
 
 

time: 589 us -> 542 us (0.920)
  the two profiles are of different devices: /device:TPU:30 before, /device:TPU:1 now
where the time goes in v1:
time: 542 us; the launch traced here: 541 us
  starting transfers between devices  233 us (43%)
  waiting for transfers between devices  203 us (37%)
  other arithmetic  51.9 us (10%)
  blocking collectives  41.6 us (8%)
  matrix products  6.14 us (1%)
    ppermute x40, starting transfers between devices, passed_along(): lax.ppermute(array, axis, [(i, (i + by) % length) for i in range(length)])  233 us
    ppermute x40, waiting for transfers between devices, passed_along(): lax.ppermute(array, axis, [(i, (i + by) % length) for i in range(length)])  203 us
    all_gather x1, blocking collectives, local(): lax.all_gather(jnp.sum(products, axis=0), 'ctx')  41.6 us
    another operation x1, other arithmetic, forward_step(): jnp.cumsum(growth * segment[:, None, :], axis=0)  29.8 us
    another operation x1, other arithmetic, backward_step(): lax.cumsum(start_weights * segment[:, None, :], axis=0, reverse=True)  11.1 us
  transfers between devices with their start and end apart: 40, of which 35 were waited for; matrix products, arithmetic and copies ran while one was open for 3% of the time, Pallas kernels for 0%

profile of v1, /device:TPU:1, one launch (start us, length us, event | category | flops | bytes accessed | tf_op | source)
XLA Modules:
  0.0 540.7 jit_solution(16508584409205461974)
XLA Ops:
  8.5 11.1 %fusion.2 = f32[128,16,512]{2,1,0:T(8,128)} fusion(f32[128,512]{1,0:T(8,128)S(1)} %get-tuple-element.156, f32[16,512]{1,0:T(8,128)S(1)} %get-tuple-element.168), kind=kOutput, calls=%fused_computation.10 | output fusion | flops 135266304 | bytes 4489216 | tf_op jit(solution)/shard_map/while/body/eval_jaxpr/reduce_window_sum | solution.py:53
  29.7 10.9 %collective-permute-done.4 = bf16[2,128,512]{2,1,0:T(8,128)(2,1)S(1)} collective-permute-done((bf16[2,128,512]{2,1,0:T(8,128)(2,1)S(1)}, bf16[2,128,512]{2,1,0:T(8,128)(2,1)S(1)}, u32[]{:S(2)}, u32[]{:S(2)}) %collective-permute-start.4) | collective-permute-done | bytes 262176 | tf_op jit(solution)/shard_map/ppermute | solution.py:13
  42.8 12.1 %collective-permute-done.5 = bf16[2,128,512]{2,1,0:T(8,128)(2,1)S(1)} collective-permute-done((bf16[2,128,512]{2,1,0:T(8,128)(2,1)S(1)}, bf16[2,128,512]{2,1,0:T(8,128)(2,1)S(1)}, u32[]{:S(2)}, u32[]{:S(2)}) %collective-permute-start.5) | collective-permute-done | bytes 262176 | tf_op jit(solution)/shard_map/ppermute | solution.py:13
  60.8 191.8 %while.5 = (s32[]{:T(128)}, f32[16,512]{1,0:T(8,128)S(1)}, f32[16,512]{1,0:T(8,128)S(1)}, f32[16,512]{1,0:T(8,128)S(1)}, s32[]{:T(128)}) while((s32[]{:T(128)}, f32[16,512]{1,0:T(8,128)S(1)}, f32[16,512]{1,0:T(8,128)S(1)}, f32[16,512]{1,0:T(8,128)S(1)}, s32[]{:T(128)}) %tuple.71), condition=%wide.region_18.19_spmd, body=%wide.region_17.18_spmd.sunk | while | flops 16386 | bytes 262245 | solution.py:142
  62.8 12.0 %collective-permute-done.1 = f32[16,512]{1,0:T(8,128)S(1)} collective-permute-done((f32[16,512]{1,0:T(8,128)S(1)}, f32[16,512]{1,0:T(8,128)S(1)}, u32[]{:S(2)}, u32[]{:S(2)}) %collective-permute-start.1) | collective-permute-done | bytes 32800 | tf_op jit(solution)/shard_map/while/body/eval_jaxpr/ppermute | solution.py:13
  219.0 9.9 %collective-permute-done.1 = f32[16,512]{1,0:T(8,128)S(1)} collective-permute-done((f32[16,512]{1,0:T(8,128)S(1)}, f32[16,512]{1,0:T(8,128)S(1)}, u32[]{:S(2)}, u32[]{:S(2)}) %collective-permute-start.1) | collective-permute-done | bytes 32800 | tf_op jit(solution)/shard_map/while/body/eval_jaxpr/ppermute | solution.py:13
  252.6 181.4 %while.4 = (s32[]{:T(128)}, f32[16,512]{1,0:T(8,128)S(1)}, f32[16,512]{1,0:T(8,128)S(1)}, f32[16,512]{1,0:T(8,128)S(1)}, s32[]{:T(128)}) while((s32[]{:T(128)}, f32[16,512]{1,0:T(8,128)S(1)}, f32[16,512]{1,0:T(8,128)S(1)}, f32[16,512]{1,0:T(8,128)S(1)}, s32[]{:T(128)}) %tuple.74), condition=%wide.region_4.0_spmd, body=%wide.region_3.4_spmd.sunk | while | flops 16386 | bytes 262245 | solution.py:50
  252.6 11.1 %collective-permute-start = (f32[16,512]{1,0:T(8,128)S(1)}, f32[16,512]{1,0:T(8,128)S(1)}, u32[]{:S(2)}, u32[]{:S(2)}) collective-permute-start(f32[16,512]{1,0:T(8,128)S(1)} %multiply_add_fusion.5), channel_id=1, source_target_pairs={{0,480},{32,0},{64,32},{96,64},{128,96},{160,128},{192,160},{224,1... | collective-permute-start | bytes 98312 | tf_op jit(solution)/shard_map/while/body/eval_jaxpr/ppermute | solution.py:13
  279.9 11.0 %collective-permute-start = (f32[16,512]{1,0:T(8,128)S(1)}, f32[16,512]{1,0:T(8,128)S(1)}, u32[]{:S(2)}, u32[]{:S(2)}) collective-permute-start(f32[16,512]{1,0:T(8,128)S(1)} %multiply_add_fusion.5), channel_id=1, source_target_pairs={{0,480},{32,0},{64,32},{96,64},{128,96},{160,128},{192,160},{224,1... | collective-permute-start | bytes 98312 | tf_op jit(solution)/shard_map/while/body/eval_jaxpr/ppermute | solution.py:13
  291.8 11.0 %collective-permute-start = (f32[16,512]{1,0:T(8,128)S(1)}, f32[16,512]{1,0:T(8,128)S(1)}, u32[]{:S(2)}, u32[]{:S(2)}) collective-permute-start(f32[16,512]{1,0:T(8,128)S(1)} %multiply_add_fusion.5), channel_id=1, source_target_pairs={{0,480},{32,0},{64,32},{96,64},{128,96},{160,128},{192,160},{224,1... | collective-permute-start | bytes 98312 | tf_op jit(solution)/shard_map/while/body/eval_jaxpr/ppermute | solution.py:13
  303.6 11.0 %collective-permute-start = (f32[16,512]{1,0:T(8,128)S(1)}, f32[16,512]{1,0:T(8,128)S(1)}, u32[]{:S(2)}, u32[]{:S(2)}) collective-permute-start(f32[16,512]{1,0:T(8,128)S(1)} %multiply_add_fusion.5), channel_id=1, source_target_pairs={{0,480},{32,0},{64,32},{96,64},{128,96},{160,128},{192,160},{224,1... | collective-permute-start | bytes 98312 | tf_op jit(solution)/shard_map/while/body/eval_jaxpr/ppermute | solution.py:13
  315.5 11.0 %collective-permute-start = (f32[16,512]{1,0:T(8,128)S(1)}, f32[16,512]{1,0:T(8,128)S(1)}, u32[]{:S(2)}, u32[]{:S(2)}) collective-permute-start(f32[16,512]{1,0:T(8,128)S(1)} %multiply_add_fusion.5), channel_id=1, source_target_pairs={{0,480},{32,0},{64,32},{96,64},{128,96},{160,128},{192,160},{224,1... | collective-permute-start | bytes 98312 | tf_op jit(solution)/shard_map/while/body/eval_jaxpr/ppermute | solution.py:13
  327.3 11.0 %collective-permute-start = (f32[16,512]{1,0:T(8,128)S(1)}, f32[16,512]{1,0:T(8,128)S(1)}, u32[]{:S(2)}, u32[]{:S(2)}) collective-permute-start(f32[16,512]{1,0:T(8,128)S(1)} %multiply_add_fusion.5), channel_id=1, source_target_pairs={{0,480},{32,0},{64,32},{96,64},{128,96},{160,128},{192,160},{224,1... | collective-permute-start | bytes 98312 | tf_op jit(solution)/shard_map/while/body/eval_jaxpr/ppermute | solution.py:13
  339.2 11.0 %collective-permute-start = (f32[16,512]{1,0:T(8,128)S(1)}, f32[16,512]{1,0:T(8,128)S(1)}, u32[]{:S(2)}, u32[]{:S(2)}) collective-permute-start(f32[16,512]{1,0:T(8,128)S(1)} %multiply_add_fusion.5), channel_id=1, source_target_pairs={{0,480},{32,0},{64,32},{96,64},{128,96},{160,128},{192,160},{224,1... | collective-permute-start | bytes 98312 | tf_op jit(solution)/shard_map/while/body/eval_jaxpr/ppermute | solution.py:13
  351.1 11.0 %collective-permute-start = (f32[16,512]{1,0:T(8,128)S(1)}, f32[16,512]{1,0:T(8,128)S(1)}, u32[]{:S(2)}, u32[]{:S(2)}) collective-permute-start(f32[16,512]{1,0:T(8,128)S(1)} %multiply_add_fusion.5), channel_id=1, source_target_pairs={{0,480},{32,0},{64,32},{96,64},{128,96},{160,128},{192,160},{224,1... | collective-permute-start | bytes 98312 | tf_op jit(solution)/shard_map/while/body/eval_jaxpr/ppermute | solution.py:13
  362.9 11.0 %collective-permute-start = (f32[16,512]{1,0:T(8,128)S(1)}, f32[16,512]{1,0:T(8,128)S(1)}, u32[]{:S(2)}, u32[]{:S(2)}) collective-permute-start(f32[16,512]{1,0:T(8,128)S(1)} %multiply_add_fusion.5), channel_id=1, source_target_pairs={{0,480},{32,0},{64,32},{96,64},{128,96},{160,128},{192,160},{224,1... | collective-permute-start | bytes 98312 | tf_op jit(solution)/shard_map/while/body/eval_jaxpr/ppermute | solution.py:13
  374.8 11.0 %collective-permute-start = (f32[16,512]{1,0:T(8,128)S(1)}, f32[16,512]{1,0:T(8,128)S(1)}, u32[]{:S(2)}, u32[]{:S(2)}) collective-permute-start(f32[16,512]{1,0:T(8,128)S(1)} %multiply_add_fusion.5), channel_id=1, source_target_pairs={{0,480},{32,0},{64,32},{96,64},{128,96},{160,128},{192,160},{224,1... | collective-permute-start | bytes 98312 | tf_op jit(solution)/shard_map/while/body/eval_jaxpr/ppermute | solution.py:13
  386.6 11.0 %collective-permute-start = (f32[16,512]{1,0:T(8,128)S(1)}, f32[16,512]{1,0:T(8,128)S(1)}, u32[]{:S(2)}, u32[]{:S(2)}) collective-permute-start(f32[16,512]{1,0:T(8,128)S(1)} %multiply_add_fusion.5), channel_id=1, source_target_pairs={{0,480},{32,0},{64,32},{96,64},{128,96},{160,128},{192,160},{224,1... | collective-permute-start | bytes 98312 | tf_op jit(solution)/shard_map/while/body/eval_jaxpr/ppermute | solution.py:13
  398.5 11.0 %collective-permute-start = (f32[16,512]{1,0:T(8,128)S(1)}, f32[16,512]{1,0:T(8,128)S(1)}, u32[]{:S(2)}, u32[]{:S(2)}) collective-permute-start(f32[16,512]{1,0:T(8,128)S(1)} %multiply_add_fusion.5), channel_id=1, source_target_pairs={{0,480},{32,0},{64,32},{96,64},{128,96},{160,128},{192,160},{224,1... | collective-permute-start | bytes 98312 | tf_op jit(solution)/shard_map/while/body/eval_jaxpr/ppermute | solution.py:13
  410.3 11.0 %collective-permute-start = (f32[16,512]{1,0:T(8,128)S(1)}, f32[16,512]{1,0:T(8,128)S(1)}, u32[]{:S(2)}, u32[]{:S(2)}) collective-permute-start(f32[16,512]{1,0:T(8,128)S(1)} %multiply_add_fusion.5), channel_id=1, source_target_pairs={{0,480},{32,0},{64,32},{96,64},{128,96},{160,128},{192,160},{224,1... | collective-permute-start | bytes 98312 | tf_op jit(solution)/shard_map/while/body/eval_jaxpr/ppermute | solution.py:13
  422.2 11.0 %collective-permute-start = (f32[16,512]{1,0:T(8,128)S(1)}, f32[16,512]{1,0:T(8,128)S(1)}, u32[]{:S(2)}, u32[]{:S(2)}) collective-permute-start(f32[16,512]{1,0:T(8,128)S(1)} %multiply_add_fusion.5), channel_id=1, source_target_pairs={{0,480},{32,0},{64,32},{96,64},{128,96},{160,128},{192,160},{224,1... | collective-permute-start | bytes 98312 | tf_op jit(solution)/shard_map/while/body/eval_jaxpr/ppermute | solution.py:13
  434.1 29.8 %multiply_reduce_fusion.2 = (f32[16,512]{1,0:T(8,128)S(1)}, f32[128,512]{1,0:T(8,128)S(1)}, f32[128,512]{1,0:T(8,128)S(1)}) fusion(f32[16,512]{1,0:T(8,128)S(1)} %get-tuple-element.165, f32[128,512]{1,0:T(8,128)S(1)} %get-tuple-element.156, f32[16,512]{1,0:T(8,128)S(1)} %get-tuple-element.164, f32[16,512]{1,0:T(8,128)S(1)} %get-tuple-element.162, ...), kind=kOutput, calls=%fused_computation.4 | output fusion | flops 152952832 | bytes 5473280 | tf_op jit(solution)/shard_map/while/body/eval_jaxpr/jit(cumsum)/reduce_window_sum | solution.py:147
  470.2 11.0 %collective-permute-start.6 = (bf16[2,128,512]{1,2,0:T(8,128)(2,1)}, bf16[2,128,512]{1,2,0:T(8,128)(2,1)S(1)}, u32[]{:S(2)}, u32[]{:S(2)}) collective-permute-start(bf16[2,128,512]{1,2,0:T(8,128)(2,1)} %get-tuple-element.148), channel_id=1, source_target_pairs={{0,480},{32,0},{64,32},{96,64},{128,96},{160,128},{192,160},{224,1... | collective-permute-start | bytes 786440 | tf_op jit(solution)/shard_map/ppermute | solution.py:13
  495.7 41.6 %all-gather = f32[256,512]{1,0:T(8,128)S(1)} all-gather(f32[16,512]{1,0:T(8,128)S(1)} %get-tuple-element.127), channel_id=2, replica_groups=mesh['ctx'=16,'head'=8,'dp'=4] {'ctx'}, dimensions={0}, use_global_device_ids=true | all-gather | bytes 557056 | tf_op jit(solution)/shard_map/all_gather | solution.py:159
  (191 shorter events, 246.5 us)
Async XLA Ops:
  1.7 17.9 %collective-permute-start.2 = (bf16[2,128,512]{2,1,0:T(8,128)(2,1)S(1)}, bf16[2,128,512]{2,1,0:T(8,128)(2,1)S(1)}, u32[]{:S(2)}, u32[]{:S(2)}) collective-permute-start(bf16[2,128,512]{2,1,0:T(8,128)(2,1)S(1)} %pad_maximum_fusion.1), channel_id=1, source_target_pairs={{0,32},{32,64},{64,96},{96,128},{128,160},{160,192},{192,224},{224... | collective-permute-start | bytes 786440 | tf_op jit(solution)/shard_map/ppermute | solution.py:13
  26.4 14.3 %collective-permute-start.4 = (bf16[2,128,512]{2,1,0:T(8,128)(2,1)S(1)}, bf16[2,128,512]{2,1,0:T(8,128)(2,1)S(1)}, u32[]{:S(2)}, u32[]{:S(2)}) collective-permute-start(bf16[2,128,512]{2,1,0:T(8,128)(2,1)S(1)} %collective-permute-done.3), channel_id=1, source_target_pairs={{0,32},{32,64},{64,96},{96,128},{128,160},{160,192},{192,224},{224... | collective-permute-start | bytes 786440 | tf_op jit(solution)/shard_map/ppermute | solution.py:13
  40.7 14.3 %collective-permute-start.5 = (bf16[2,128,512]{2,1,0:T(8,128)(2,1)S(1)}, bf16[2,128,512]{2,1,0:T(8,128)(2,1)S(1)}, u32[]{:S(2)}, u32[]{:S(2)}) collective-permute-start(bf16[2,128,512]{2,1,0:T(8,128)(2,1)S(1)} %collective-permute-done.4), channel_id=1, source_target_pairs={{0,32},{32,64},{64,96},{96,128},{128,160},{160,192},{192,224},{224... | collective-permute-start | bytes 786440 | tf_op jit(solution)/shard_map/ppermute | solution.py:13
  60.8 14.0 %collective-permute-start.1 = (f32[16,512]{1,0:T(8,128)S(1)}, f32[16,512]{1,0:T(8,128)S(1)}, u32[]{:S(2)}, u32[]{:S(2)}) collective-permute-start(f32[16,512]{1,0:T(8,128)S(1)} %multiply_add_fusion.6), channel_id=1, source_target_pairs={{0,32},{32,64},{64,96},{96,128},{128,160},{160,192},{192,224},{224... | collective-permute-start | bytes 98312 | tf_op jit(solution)/shard_map/while/body/eval_jaxpr/ppermute | solution.py:13
  74.8 11.8 %collective-permute-start.1 = (f32[16,512]{1,0:T(8,128)S(1)}, f32[16,512]{1,0:T(8,128)S(1)}, u32[]{:S(2)}, u32[]{:S(2)}) collective-permute-start(f32[16,512]{1,0:T(8,128)S(1)} %multiply_add_fusion.6), channel_id=1, source_target_pairs={{0,32},{32,64},{64,96},{96,128},{128,160},{160,192},{192,224},{224... | collective-permute-start | bytes 98312 | tf_op jit(solution)/shard_map/while/body/eval_jaxpr/ppermute | solution.py:13
  217.0 11.8 %collective-permute-start.1 = (f32[16,512]{1,0:T(8,128)S(1)}, f32[16,512]{1,0:T(8,128)S(1)}, u32[]{:S(2)}, u32[]{:S(2)}) collective-permute-start(f32[16,512]{1,0:T(8,128)S(1)} %multiply_add_fusion.6), channel_id=1, source_target_pairs={{0,32},{32,64},{64,96},{96,128},{128,160},{160,192},{192,224},{224... | collective-permute-start | bytes 98312 | tf_op jit(solution)/shard_map/while/body/eval_jaxpr/ppermute | solution.py:13
  252.6 12.0 %collective-permute-start = (f32[16,512]{1,0:T(8,128)S(1)}, f32[16,512]{1,0:T(8,128)S(1)}, u32[]{:S(2)}, u32[]{:S(2)}) collective-permute-start(f32[16,512]{1,0:T(8,128)S(1)} %multiply_add_fusion.5), channel_id=1, source_target_pairs={{0,480},{32,0},{64,32},{96,64},{128,96},{160,128},{192,160},{224,1... | collective-permute-start | bytes 98312 | tf_op jit(solution)/shard_map/while/body/eval_jaxpr/ppermute | solution.py:13
  279.9 11.8 %collective-permute-start = (f32[16,512]{1,0:T(8,128)S(1)}, f32[16,512]{1,0:T(8,128)S(1)}, u32[]{:S(2)}, u32[]{:S(2)}) collective-permute-start(f32[16,512]{1,0:T(8,128)S(1)} %multiply_add_fusion.5), channel_id=1, source_target_pairs={{0,480},{32,0},{64,32},{96,64},{128,96},{160,128},{192,160},{224,1... | collective-permute-start | bytes 98312 | tf_op jit(solution)/shard_map/while/body/eval_jaxpr/ppermute | solution.py:13
  291.8 11.8 %collective-permute-start = (f32[16,512]{1,0:T(8,128)S(1)}, f32[16,512]{1,0:T(8,128)S(1)}, u32[]{:S(2)}, u32[]{:S(2)}) collective-permute-start(f32[16,512]{1,0:T(8,128)S(1)} %multiply_add_fusion.5), channel_id=1, source_target_pairs={{0,480},{32,0},{64,32},{96,64},{128,96},{160,128},{192,160},{224,1... | collective-permute-start | bytes 98312 | tf_op jit(solution)/shard_map/while/body/eval_jaxpr/ppermute | solution.py:13
  303.6 11.8 %collective-permute-start = (f32[16,512]{1,0:T(8,128)S(1)}, f32[16,512]{1,0:T(8,128)S(1)}, u32[]{:S(2)}, u32[]{:S(2)}) collective-permute-start(f32[16,512]{1,0:T(8,128)S(1)} %multiply_add_fusion.5), channel_id=1, source_target_pairs={{0,480},{32,0},{64,32},{96,64},{128,96},{160,128},{192,160},{224,1... | collective-permute-start | bytes 98312 | tf_op jit(solution)/shard_map/while/body/eval_jaxpr/ppermute | solution.py:13
  315.5 11.8 %collective-permute-start = (f32[16,512]{1,0:T(8,128)S(1)}, f32[16,512]{1,0:T(8,128)S(1)}, u32[]{:S(2)}, u32[]{:S(2)}) collective-permute-start(f32[16,512]{1,0:T(8,128)S(1)} %multiply_add_fusion.5), channel_id=1, source_target_pairs={{0,480},{32,0},{64,32},{96,64},{128,96},{160,128},{192,160},{224,1... | collective-permute-start | bytes 98312 | tf_op jit(solution)/shard_map/while/body/eval_jaxpr/ppermute | solution.py:13
  327.3 11.8 %collective-permute-start = (f32[16,512]{1,0:T(8,128)S(1)}, f32[16,512]{1,0:T(8,128)S(1)}, u32[]{:S(2)}, u32[]{:S(2)}) collective-permute-start(f32[16,512]{1,0:T(8,128)S(1)} %multiply_add_fusion.5), channel_id=1, source_target_pairs={{0,480},{32,0},{64,32},{96,64},{128,96},{160,128},{192,160},{224,1... | collective-permute-start | bytes 98312 | tf_op jit(solution)/shard_map/while/body/eval_jaxpr/ppermute | solution.py:13
  339.2 11.8 %collective-permute-start = (f32[16,512]{1,0:T(8,128)S(1)}, f32[16,512]{1,0:T(8,128)S(1)}, u32[]{:S(2)}, u32[]{:S(2)}) collective-permute-start(f32[16,512]{1,0:T(8,128)S(1)} %multiply_add_fusion.5), channel_id=1, source_target_pairs={{0,480},{32,0},{64,32},{96,64},{128,96},{160,128},{192,160},{224,1... | collective-permute-start | bytes 98312 | tf_op jit(solution)/shard_map/while/body/eval_jaxpr/ppermute | solution.py:13
  351.1 11.8 %collective-permute-start = (f32[16,512]{1,0:T(8,128)S(1)}, f32[16,512]{1,0:T(8,128)S(1)}, u32[]{:S(2)}, u32[]{:S(2)}) collective-permute-start(f32[16,512]{1,0:T(8,128)S(1)} %multiply_add_fusion.5), channel_id=1, source_target_pairs={{0,480},{32,0},{64,32},{96,64},{128,96},{160,128},{192,160},{224,1... | collective-permute-start | bytes 98312 | tf_op jit(solution)/shard_map/while/body/eval_jaxpr/ppermute | solution.py:13
  362.9 11.8 %collective-permute-start = (f32[16,512]{1,0:T(8,128)S(1)}, f32[16,512]{1,0:T(8,128)S(1)}, u32[]{:S(2)}, u32[]{:S(2)}) collective-permute-start(f32[16,512]{1,0:T(8,128)S(1)} %multiply_add_fusion.5), channel_id=1, source_target_pairs={{0,480},{32,0},{64,32},{96,64},{128,96},{160,128},{192,160},{224,1... | collective-permute-start | bytes 98312 | tf_op jit(solution)/shard_map/while/body/eval_jaxpr/ppermute | solution.py:13
  374.8 11.8 %collective-permute-start = (f32[16,512]{1,0:T(8,128)S(1)}, f32[16,512]{1,0:T(8,128)S(1)}, u32[]{:S(2)}, u32[]{:S(2)}) collective-permute-start(f32[16,512]{1,0:T(8,128)S(1)} %multiply_add_fusion.5), channel_id=1, source_target_pairs={{0,480},{32,0},{64,32},{96,64},{128,96},{160,128},{192,160},{224,1... | collective-permute-start | bytes 98312 | tf_op jit(solution)/shard_map/while/body/eval_jaxpr/ppermute | solution.py:13
  386.6 11.8 %collective-permute-start = (f32[16,512]{1,0:T(8,128)S(1)}, f32[16,512]{1,0:T(8,128)S(1)}, u32[]{:S(2)}, u32[]{:S(2)}) collective-permute-start(f32[16,512]{1,0:T(8,128)S(1)} %multiply_add_fusion.5), channel_id=1, source_target_pairs={{0,480},{32,0},{64,32},{96,64},{128,96},{160,128},{192,160},{224,1... | collective-permute-start | bytes 98312 | tf_op jit(solution)/shard_map/while/body/eval_jaxpr/ppermute | solution.py:13
  398.5 11.8 %collective-permute-start = (f32[16,512]{1,0:T(8,128)S(1)}, f32[16,512]{1,0:T(8,128)S(1)}, u32[]{:S(2)}, u32[]{:S(2)}) collective-permute-start(f32[16,512]{1,0:T(8,128)S(1)} %multiply_add_fusion.5), channel_id=1, source_target_pairs={{0,480},{32,0},{64,32},{96,64},{128,96},{160,128},{192,160},{224,1... | collective-permute-start | bytes 98312 | tf_op jit(solution)/shard_map/while/body/eval_jaxpr/ppermute | solution.py:13
  410.3 11.8 %collective-permute-start = (f32[16,512]{1,0:T(8,128)S(1)}, f32[16,512]{1,0:T(8,128)S(1)}, u32[]{:S(2)}, u32[]{:S(2)}) collective-permute-start(f32[16,512]{1,0:T(8,128)S(1)} %multiply_add_fusion.5), channel_id=1, source_target_pairs={{0,480},{32,0},{64,32},{96,64},{128,96},{160,128},{192,160},{224,1... | collective-permute-start | bytes 98312 | tf_op jit(solution)/shard_map/while/body/eval_jaxpr/ppermute | solution.py:13
  422.2 11.8 %collective-permute-start = (f32[16,512]{1,0:T(8,128)S(1)}, f32[16,512]{1,0:T(8,128)S(1)}, u32[]{:S(2)}, u32[]{:S(2)}) collective-permute-start(f32[16,512]{1,0:T(8,128)S(1)} %multiply_add_fusion.5), channel_id=1, source_target_pairs={{0,480},{32,0},{64,32},{96,64},{128,96},{160,128},{192,160},{224,1... | collective-permute-start | bytes 98312 | tf_op jit(solution)/shard_map/while/body/eval_jaxpr/ppermute | solution.py:13
  470.2 67.8 %collective-permute-start.6 = (bf16[2,128,512]{1,2,0:T(8,128)(2,1)}, bf16[2,128,512]{1,2,0:T(8,128)(2,1)S(1)}, u32[]{:S(2)}, u32[]{:S(2)}) collective-permute-start(bf16[2,128,512]{1,2,0:T(8,128)(2,1)} %get-tuple-element.148), channel_id=1, source_target_pairs={{0,480},{32,0},{64,32},{96,64},{128,96},{160,128},{192,160},{224,1... | collective-permute-start | bytes 786440 | tf_op jit(solution)/shard_map/ppermute | solution.py:13
  481.2 56.8 %collective-permute-start.7 = (bf16[2,128,512]{1,2,0:T(8,128)(2,1)S(1)}, bf16[2,128,512]{1,2,0:T(8,128)(2,1)S(1)}, u32[]{:S(2)}, u32[]{:S(2)}) collective-permute-start(bf16[2,128,512]{1,2,0:T(8,128)(2,1)S(1)} %get-tuple-element.149), channel_id=1, source_target_pairs={{0,448},{32,480},{64,0},{96,32},{128,64},{160,96},{192,128},{224,1... | collective-permute-start | bytes 786440 | tf_op jit(solution)/shard_map/ppermute | solution.py:13
  491.0 47.0 %collective-permute-start.8 = (bf16[2,128,512]{1,2,0:T(8,128)(2,1)S(1)}, bf16[2,128,512]{1,2,0:T(8,128)(2,1)S(1)}, u32[]{:S(2)}, u32[]{:S(2)}) collective-permute-start(bf16[2,128,512]{1,2,0:T(8,128)(2,1)S(1)} %get-tuple-element.151), channel_id=1, source_target_pairs={{0,416},{32,448},{64,480},{96,0},{128,32},{160,64},{192,96},{224,1... | collective-permute-start | bytes 786440 | tf_op jit(solution)/shard_map/ppermute | solution.py:13
  493.0 45.0 %collective-permute-start.9 = (bf16[2,128,512]{1,2,0:T(8,128)(2,1)S(1)}, bf16[2,128,512]{1,2,0:T(8,128)(2,1)}, u32[]{:S(2)}, u32[]{:S(2)}) collective-permute-start(bf16[2,128,512]{1,2,0:T(8,128)(2,1)S(1)} %get-tuple-element.150), channel_id=1, source_target_pairs={{0,384},{32,416},{64,448},{96,480},{128,0},{160,32},{192,64},{224,... | collective-permute-start | bytes 786440 | tf_op jit(solution)/shard_map/ppermute | solution.py:13
  (34 other events, 867.6 us)
